TPU v7x, 256 devices: a whole 4x4x8 slice. The times are simulated.
256 devices in a mesh: loop: 16 (over z, y_lo), rep: 16 (over y_hi, x, core).
Axes of the slice: x: 4, y: 4 (y_hi: 2, y_lo: 2; y = y_hi * 2 + y_lo), z: 8, core: 2. Of those that a mesh axis runs over, the one named last changes fastest.
Arguments:
- features: bfloat16 [65536, 128], P(('loop', 'rep')), may hold values from -6 to 6
- w_self: bfloat16 [128, 256], replicated, may hold values from -0.5 to 0.5
- w_neigh: bfloat16 [128, 256], replicated, may hold values from -0.5 to 0.5
- bias: float32 [256], replicated, may hold values from -3 to 3
- degree: int32 [65536], P(('loop', 'rep')), may hold values from 1 to 4
- tiles: bfloat16 [16, 16, 16, 16, 128, 128], P('loop', 'rep'), may hold values from -0.0625 to 0.0625
- dst_block: int32 [16, 16, 16, 16], P('loop', 'rep'), may hold values from 0 to 31, as said below
- src_block: int32 [16, 16, 16, 16], P('loop', 'rep'), may hold values from 0 to 1, as said below
- live_count: int32 [16, 16, 16], P('loop', 'rep'), may hold values from 1 to 16, as said below
- cotangent: bfloat16 [65536, 256], P(('loop', 'rep')), may hold values from -6 to 6
Outputs:
- output: bfloat16 [65536, 256], P(('loop', 'rep'))
- grad_input: bfloat16 [65536, 128], P(('loop', 'rep'))
- grad_self: float32 [128, 256], replicated
- grad_neigh: float32 [128, 256], replicated
- grad_bias: float32 [256], replicated
Inputs may be any that keep to these rules, and one draw needn't show every extreme that they name: Within one (p, r, q) the 16 slots name distinct pairs (dst_block, src_block). Within one (p, r, q) the 16 slots name distinct pairs (dst_block, src_block). `live_count`: every device (p, r) has some q with all 16 slots live; slots at or past the count hold tiles that are not part of the graph.
All inputs are finite; a program needn't handle non-finite values.
Results may differ from a plain program's by a relative error of at most 0.0075.
Values may be sent and summed in bfloat16 or wider, within the bound.
A program may use at most 128 MiB of HBM per device.

v0:
```python
import math
import jax
import jax.numpy as jnp
from jax import lax
from jax.sharding import PartitionSpec as P


def shifted(block, axis, distance):
    devices = range(lax.axis_size(axis))
    route = [((i - distance) % len(devices), i) for i in devices]
    return lax.ppermute(block, axis, route)


def per_device(
    features, w_self, w_neigh, bias, degree, tiles, dst_block, src_block, live_count, cotangent
):
    loop_count = lax.axis_size("loop")
    rep_count = lax.axis_size("rep")
    loop_here = lax.axis_index("loop")
    row_count, feat_width = features.shape
    tile_size = tiles.shape[-1]
    slot_count = tiles.shape[3]
    sub_blocks = row_count // tile_size
    row_blocks = sub_blocks * rep_count
    tile_all = tiles[0, 0]
    dst_all = dst_block[0, 0]
    src_all = src_block[0, 0]
    live_all = jnp.arange(slot_count)[None, :] < live_count[0, 0][:, None]
    place_all = (
        (dst_all[:, :, None] == jnp.arange(row_blocks)[None, None, :]) & live_all[:, :, None]
    ).astype(jnp.float32)
    land_all = (
        (src_all[:, :, None] == jnp.arange(sub_blocks)[None, None, :]) & live_all[:, :, None]
    ).astype(jnp.float32)

    def pick_entry(table, source):
        return lax.dynamic_index_in_dim(table, source, 0, keepdims=False)

    def gather_term(source, panel):
        tile_part = pick_entry(tile_all, source)
        chosen = jnp.take(
            panel.reshape(sub_blocks, tile_size, feat_width), pick_entry(src_all, source), axis=0
        )
        product = jnp.einsum("tij,tjf->tif", tile_part, chosen, preferred_element_type=jnp.float32)
        return jnp.einsum(
            "td,tif->dif", pick_entry(place_all, source), product, precision=lax.Precision.HIGHEST
        )

    running = gather_term(loop_here, features)

    def one_way(step_index, state):
        panel, total = state
        panel = shifted(panel, "loop", 1)
        return (panel, total + gather_term((loop_here - step_index) % loop_count, panel))

    _, running = lax.fori_loop(1, loop_count, one_way, (features, running))
    agg_sum = lax.psum_scatter(
        running.reshape(row_blocks * tile_size, feat_width), "rep", scatter_dimension=0, tiled=True
    )
    degree_f = degree.astype(jnp.float32)[:, None]
    aggregate = (agg_sum / degree_f).astype(jnp.bfloat16)
    preact = (
        jnp.dot(features, w_self, preferred_element_type=jnp.float32)
        + jnp.dot(aggregate, w_neigh, preferred_element_type=jnp.float32)
        + bias
    )
    sigmoid_val = jax.nn.sigmoid(preact)
    output = (preact * sigmoid_val).astype(jnp.bfloat16)
    grad_pre = (
        cotangent.astype(jnp.float32) * sigmoid_val * (1.0 + preact * (1.0 - sigmoid_val))
    ).astype(jnp.bfloat16)
    grad_agg = (
        jnp.einsum("nh,fh->nf", grad_pre, w_neigh, preferred_element_type=jnp.float32) / degree_f
    ).astype(jnp.bfloat16)
    grad_whole = lax.all_gather(grad_agg, "rep", axis=0, tiled=True).reshape(
        row_blocks, tile_size, feat_width
    )
    node_total = row_count * loop_count * rep_count
    grad_scale = 1.0 / math.sqrt(node_total)
    grad_self, grad_neigh, grad_bias = lax.psum(
        (
            jnp.einsum("nf,nh->fh", features, grad_pre, preferred_element_type=jnp.float32)
            * grad_scale,
            jnp.einsum("nf,nh->fh", aggregate, grad_pre, preferred_element_type=jnp.float32)
            * grad_scale,
            jnp.sum(grad_pre.astype(jnp.float32), axis=0) * grad_scale,
        ),
        ("loop", "rep"),
    )
    self_grad = jnp.einsum("nh,fh->nf", grad_pre, w_self, preferred_element_type=jnp.float32)

    def spread_term(source):
        tile_part = pick_entry(tile_all, source)
        chosen = jnp.take(grad_whole, pick_entry(dst_all, source), axis=0)
        product = jnp.einsum("tij,tif->tjf", tile_part, chosen, preferred_element_type=jnp.float32)
        summed = jnp.einsum(
            "ts,tjf->sjf", pick_entry(land_all, source), product, precision=lax.Precision.HIGHEST
        )
        return summed.reshape(row_count, feat_width)

    def carry_along(step_index, total):
        total = shifted(total, "loop", -1)
        return total + spread_term((loop_here + 1 + step_index) % loop_count)

    neigh_grad = lax.fori_loop(
        1, loop_count, carry_along, spread_term((loop_here + 1) % loop_count)
    )
    grad_input = (self_grad + neigh_grad).astype(jnp.bfloat16)
    return (output, grad_input, grad_self, grad_neigh, grad_bias)


def solution(mesh):
    in_specs = (
        P(("loop", "rep"), None),
        P(),
        P(),
        P(),
        P(("loop", "rep")),
        P("loop", "rep", None, None, None, None),
        P("loop", "rep", None, None),
        P("loop", "rep", None, None),
        P("loop", "rep", None),
        P(("loop", "rep"), None),
    )
    out_specs = (P(("loop", "rep"), None), P(("loop", "rep"), None), P(), P(), P())
    return jax.shard_map(
        per_device, mesh=mesh, in_specs=in_specs, out_specs=out_specs, check_vma=False
    )
```

profile of v0, /device:TPU:2, one launch (start us, length us, event | category | flops | bytes accessed | tf_op | source)
XLA Modules:
  0.0 704.0 jit_solution(3189512164626604518)
XLA Ops:
  9.5 1.5 gather_fusion.2
  13.3 1.5 fusion.33
  14.8 174.0 %while.32 = (s32[]{:T(128)}, bf16[256,128]{1,0:T(8,128)(2,1)S(1)}, f32[32,128,128]{2,0,1:T(8,128)S(1)}, s32[]{:T(128)}, f32[16,16,32]{2,1,0:T(8,128)S(1)}, /*ind...) while((s32[]{:T(128)}, bf16[256,128]{1,0:T(8,128)(2,1)S(1)}, ...), condition=%wide.region_1.3_spmd, body=%wide.region_0.2_spmd.sunk | while | flops 168559728 | bytes 8794716 | solution.py:56
  14.8 1.7 collective-permute-start
  16.5 7.5 %collective-permute-done = bf16[256,128]{1,0:T(8,128)(2,1)S(1)} collective-permute-done((bf16[256,128]{1,0:T(8,128)(2,1)S(1)}, bf16[256,128]{1,0:T(8,128)(2,1)S(1)}, u32[]{:S(2)}, u32[]{:S(2)}) %collective-permute-start) | collective-permute-done | bytes 65568 | tf_op jit(solution)/shard_map/while/body/eval_jaxpr/ppermute | solution.py:11
  26.1 2.8 convolution_add_fusion.4
  29.1 6.3 collective-permute-done
  37.5 2.8 convolution_add_fusion.4
  40.5 6.3 collective-permute-done
  48.8 2.8 convolution_add_fusion.4
  51.8 6.3 collective-permute-done
  60.2 2.8 convolution_add_fusion.4
  63.2 6.3 collective-permute-done
  71.6 2.8 convolution_add_fusion.4
  74.6 6.3 collective-permute-done
  83.0 2.8 convolution_add_fusion.4
  86.0 6.3 collective-permute-done
  94.4 2.8 convolution_add_fusion.4
  97.4 6.3 collective-permute-done
  105.8 2.8 convolution_add_fusion.4
  108.8 6.8 collective-permute-done
  117.7 2.8 convolution_add_fusion.4
  120.7 6.3 collective-permute-done
  129.0 2.8 convolution_add_fusion.4
  132.0 6.3 collective-permute-done
  140.4 2.8 convolution_add_fusion.4
  143.4 6.3 collective-permute-done
  151.8 2.8 convolution_add_fusion.4
  154.8 6.3 collective-permute-done
  163.2 2.8 convolution_add_fusion.4
  166.2 6.3 collective-permute-done
  174.6 2.8 convolution_add_fusion.4
  177.6 6.3 collective-permute-done
  186.0 2.8 convolution_add_fusion.4
  188.8 2.6 copy.18
  192.4 77.7 %reduce-scatter.2.cloned.1.call-done = f32[256,128]{1,0:T(8,128)} async-done(((f32[4096,128]{1,0:T(8,128)}), f32[256,128]{1,0:T(8,128)}) %reduce-scatter.2.cloned.1.call-update) | async-done | bytes 131088 | tf_op jit(solution)/shard_map/reduce_scatter | solution.py:57
  270.1 2.0 convert_reduce_fusion
  275.6 74.1 %psum.23 = f32[256]{0:T(256)} all-reduce(f32[256]{0:T(256)S(1)} %broadcast_multiply_fusion), channel_id=1, replica_groups=mesh['loop'=16,'rep'=16] {'loop','rep'}, use_global_device_ids=true, to_apply=%region_8.11 | all-reduce | flops 256 | bytes 2048 | tf_op jit(solution)/shard_map/psum | solution.py:80
  349.7 177.0 %all-reduce.3.cloned.1.call-done = (f32[128,256]{0,1:T(8,128)}, f32[128,256]{1,0:T(8,128)}) async-done(((f32[128,256]{0,1:T(8,128)}, f32[128,256]{1,0:T(8,128)}), (f32[128,256]{0,1:T(8,128)}, f32[128,256]{1,0:T(8,128)})) %all-reduce.3.cloned.1.call-update) | async-done | bytes 262160 | tf_op jit(solution)/shard_map/psum | solution.py:80
  526.7 1.7 copy.20
  528.4 50.3 %all-gather.2.cloned.1.call-done = bf16[4096,128]{1,0:T(8,128)(2,1)} async-done(((bf16[256,128]{1,0:T(8,128)(2,1)}), bf16[4096,128]{1,0:T(8,128)(2,1)}) %all-gather.2.cloned.1.call-update) | async-done | bytes 1048592 | tf_op jit(solution)/shard_map/all_gather | solution.py:75
  578.6 2.0 gather_fusion.3
  583.2 112.8 %while.33 = (s32[]{:T(128)}, f32[256,128]{1,0:T(8,128)S(1)}, s32[]{:T(128)}, f32[16,16,2]{1,2,0:T(2,128)S(1)}, bf16[16,16,128,128]{3,2,1,0:T(8,128)(2,1)}, /*ind...) while((s32[]{:T(128)}, f32[256,128]{1,0:T(8,128)S(1)}, ...), condition=%wide.region_4.7_spmd, body=%wide.region_3.6_spmd.sunk | while | flops 73696368 | bytes 5510748 | solution.py:105
  583.2 3.4 collective-permute-start.1
  588.0 1.4 fusion.93
  590.6 3.8 collective-permute-start.1
  598.5 3.1 collective-permute-start.1
  605.7 3.1 collective-permute-start.1
  610.2 1.4 fusion.93
  612.9 3.1 collective-permute-start.1
  617.4 1.4 fusion.93
  620.1 3.5 collective-permute-start.1
  627.6 4.5 collective-permute-start.1
  636.1 3.6 collective-permute-start.1
  641.1 1.4 fusion.93
  643.7 3.1 collective-permute-start.1
  650.9 3.1 collective-permute-start.1
  658.1 3.1 collective-permute-start.1
  665.3 3.8 collective-permute-start.1
  670.4 1.4 fusion.93
  673.1 4.2 collective-permute-start.1
  678.6 1.4 fusion.93
  681.3 3.4 collective-permute-start.1
  688.8 3.1 collective-permute-start.1
  (249 shorter events, 96.8 us)
Async XLA Ops:
  7.2 262.9 %copy-start = (bf16[128,256]{1,0:T(8,128)(2,1)S(1)}, bf16[128,256]{1,0:T(8,128)(2,1)}, u32[]{:S(2)}) copy-start(bf16[128,256]{1,0:T(8,128)(2,1)} %param.20) | copy-start | bytes 196612
  7.2 262.9 %reduce-scatter.2.cloned.1.call-start = ((), (), s32[]{:S(2)}) async-start(), calls=%async_computation.1 | async-start | bytes 2228224 | tf_op jit(solution)/shard_map/reduce_scatter | solution.py:57
  13.3 1.5 copy-start.5
  14.8 9.2 %collective-permute-start = (bf16[256,128]{1,0:T(8,128)(2,1)S(1)}, bf16[256,128]{1,0:T(8,128)(2,1)S(1)}, u32[]{:S(2)}, u32[]{:S(2)}) collective-permute-start(bf16[256,128]{1,0:T(8,128)(2,1)S(1)} %get-tuple-element.526), channel_id=1, source_target_pairs={{240,0},{0,16},{16,32},{32,48},{48,64},{64,80},{80,96},{96,112},{1... | collective-permute-start | bytes 196616 | tf_op jit(solution)/shard_map/while/body/eval_jaxpr/ppermute | solution.py:11
  28.9 6.5 collective-permute-start
  40.3 6.5 collective-permute-start
  51.7 6.5 collective-permute-start
  63.1 6.5 collective-permute-start
  74.5 6.5 collective-permute-start
  85.8 6.5 collective-permute-start
  97.2 6.5 collective-permute-start
  108.6 7.0 collective-permute-start
  120.5 6.5 collective-permute-start
  131.9 6.5 collective-permute-start
  143.3 6.5 collective-permute-start
  154.7 6.5 collective-permute-start
  166.1 6.5 collective-permute-start
  177.4 6.5 collective-permute-start
  191.4 0.7 copy-start.6
  191.4 0.9 copy-start.2
  191.4 0.9 copy-start.3
  191.4 78.7 %copy-start.7 = (bf16[256,256]{1,0:T(8,128)(2,1)S(1)}, bf16[256,256]{1,0:T(8,128)(2,1)}, u32[]{:S(2)}) copy-start(bf16[256,256]{1,0:T(8,128)(2,1)} %param.27) | copy-start | bytes 393220
  191.4 78.7 %copy-start.9 = (f32[256]{0:T(256)S(1)}, f32[256]{0:T(256)}, u32[]{:S(2)}) copy-start(f32[256]{0:T(256)} %param.21) | copy-start | bytes 3076
  191.4 335.3 %all-reduce.3.cloned.1.call-start = ((), (), s32[]{:S(2)}) async-start(), calls=%async_computation.3 | async-start | bytes 524288 | tf_op jit(solution)/shard_map/psum | solution.py:80
  270.1 2.9 copy-start.8
  273.9 304.7 %all-gather.2.cloned.1.call-start = ((), (), s32[]{:S(2)}) async-start(), calls=%async_computation.2 | async-start | bytes 1114112 | tf_op jit(solution)/shard_map/all_gather | solution.py:75
  578.6 4.5 copy-start.1
  583.2 113.6 %copy-start.4 = (f32[128,256]{1,0:T(8,128)S(1)}, f32[128,256]{1,0:T(8,128)}, u32[]{:S(2)}) copy-start(f32[128,256]{1,0:T(8,128)} %get-tuple-element.583) | copy-start | bytes 393220
  583.2 7.4 %collective-permute-start.1 = (f32[256,128]{1,0:T(8,128)S(1)}, f32[256,128]{1,0:T(8,128)S(1)}, u32[]{:S(2)}, u32[]{:S(2)}) collective-permute-start(f32[256,128]{1,0:T(8,128)S(1)} %get-tuple-element.559), channel_id=1, source_target_pairs={{16,0},{32,16},{48,32},{64,48},{80,64},{96,80},{112,96},{128,112},... | collective-permute-start | bytes 393224 | tf_op jit(solution)/shard_map/while/body/eval_jaxpr/ppermute | solution.py:11
  590.6 7.8 %collective-permute-start.1 = (f32[256,128]{1,0:T(8,128)S(1)}, f32[256,128]{1,0:T(8,128)S(1)}, u32[]{:S(2)}, u32[]{:S(2)}) collective-permute-start(f32[256,128]{1,0:T(8,128)S(1)} %get-tuple-element.559), channel_id=1, source_target_pairs={{16,0},{32,16},{48,32},{64,48},{80,64},{96,80},{112,96},{128,112},... | collective-permute-start | bytes 393224 | tf_op jit(solution)/shard_map/while/body/eval_jaxpr/ppermute | solution.py:11
  598.5 7.1 %collective-permute-start.1 = (f32[256,128]{1,0:T(8,128)S(1)}, f32[256,128]{1,0:T(8,128)S(1)}, u32[]{:S(2)}, u32[]{:S(2)}) collective-permute-start(f32[256,128]{1,0:T(8,128)S(1)} %get-tuple-element.559), channel_id=1, source_target_pairs={{16,0},{32,16},{48,32},{64,48},{80,64},{96,80},{112,96},{128,112},... | collective-permute-start | bytes 393224 | tf_op jit(solution)/shard_map/while/body/eval_jaxpr/ppermute | solution.py:11
  605.7 7.1 %collective-permute-start.1 = (f32[256,128]{1,0:T(8,128)S(1)}, f32[256,128]{1,0:T(8,128)S(1)}, u32[]{:S(2)}, u32[]{:S(2)}) collective-permute-start(f32[256,128]{1,0:T(8,128)S(1)} %get-tuple-element.559), channel_id=1, source_target_pairs={{16,0},{32,16},{48,32},{64,48},{80,64},{96,80},{112,96},{128,112},... | collective-permute-start | bytes 393224 | tf_op jit(solution)/shard_map/while/body/eval_jaxpr/ppermute | solution.py:11
  612.9 7.1 %collective-permute-start.1 = (f32[256,128]{1,0:T(8,128)S(1)}, f32[256,128]{1,0:T(8,128)S(1)}, u32[]{:S(2)}, u32[]{:S(2)}) collective-permute-start(f32[256,128]{1,0:T(8,128)S(1)} %get-tuple-element.559), channel_id=1, source_target_pairs={{16,0},{32,16},{48,32},{64,48},{80,64},{96,80},{112,96},{128,112},... | collective-permute-start | bytes 393224 | tf_op jit(solution)/shard_map/while/body/eval_jaxpr/ppermute | solution.py:11
  620.1 7.5 %collective-permute-start.1 = (f32[256,128]{1,0:T(8,128)S(1)}, f32[256,128]{1,0:T(8,128)S(1)}, u32[]{:S(2)}, u32[]{:S(2)}) collective-permute-start(f32[256,128]{1,0:T(8,128)S(1)} %get-tuple-element.559), channel_id=1, source_target_pairs={{16,0},{32,16},{48,32},{64,48},{80,64},{96,80},{112,96},{128,112},... | collective-permute-start | bytes 393224 | tf_op jit(solution)/shard_map/while/body/eval_jaxpr/ppermute | solution.py:11
  627.6 8.5 %collective-permute-start.1 = (f32[256,128]{1,0:T(8,128)S(1)}, f32[256,128]{1,0:T(8,128)S(1)}, u32[]{:S(2)}, u32[]{:S(2)}) collective-permute-start(f32[256,128]{1,0:T(8,128)S(1)} %get-tuple-element.559), channel_id=1, source_target_pairs={{16,0},{32,16},{48,32},{64,48},{80,64},{96,80},{112,96},{128,112},... | collective-permute-start | bytes 393224 | tf_op jit(solution)/shard_map/while/body/eval_jaxpr/ppermute | solution.py:11
  636.1 7.6 %collective-permute-start.1 = (f32[256,128]{1,0:T(8,128)S(1)}, f32[256,128]{1,0:T(8,128)S(1)}, u32[]{:S(2)}, u32[]{:S(2)}) collective-permute-start(f32[256,128]{1,0:T(8,128)S(1)} %get-tuple-element.559), channel_id=1, source_target_pairs={{16,0},{32,16},{48,32},{64,48},{80,64},{96,80},{112,96},{128,112},... | collective-permute-start | bytes 393224 | tf_op jit(solution)/shard_map/while/body/eval_jaxpr/ppermute | solution.py:11
  643.7 7.1 %collective-permute-start.1 = (f32[256,128]{1,0:T(8,128)S(1)}, f32[256,128]{1,0:T(8,128)S(1)}, u32[]{:S(2)}, u32[]{:S(2)}) collective-permute-start(f32[256,128]{1,0:T(8,128)S(1)} %get-tuple-element.559), channel_id=1, source_target_pairs={{16,0},{32,16},{48,32},{64,48},{80,64},{96,80},{112,96},{128,112},... | collective-permute-start | bytes 393224 | tf_op jit(solution)/shard_map/while/body/eval_jaxpr/ppermute | solution.py:11
  650.9 7.1 %collective-permute-start.1 = (f32[256,128]{1,0:T(8,128)S(1)}, f32[256,128]{1,0:T(8,128)S(1)}, u32[]{:S(2)}, u32[]{:S(2)}) collective-permute-start(f32[256,128]{1,0:T(8,128)S(1)} %get-tuple-element.559), channel_id=1, source_target_pairs={{16,0},{32,16},{48,32},{64,48},{80,64},{96,80},{112,96},{128,112},... | collective-permute-start | bytes 393224 | tf_op jit(solution)/shard_map/while/body/eval_jaxpr/ppermute | solution.py:11
  658.1 7.1 %collective-permute-start.1 = (f32[256,128]{1,0:T(8,128)S(1)}, f32[256,128]{1,0:T(8,128)S(1)}, u32[]{:S(2)}, u32[]{:S(2)}) collective-permute-start(f32[256,128]{1,0:T(8,128)S(1)} %get-tuple-element.559), channel_id=1, source_target_pairs={{16,0},{32,16},{48,32},{64,48},{80,64},{96,80},{112,96},{128,112},... | collective-permute-start | bytes 393224 | tf_op jit(solution)/shard_map/while/body/eval_jaxpr/ppermute | solution.py:11
  665.3 7.8 %collective-permute-start.1 = (f32[256,128]{1,0:T(8,128)S(1)}, f32[256,128]{1,0:T(8,128)S(1)}, u32[]{:S(2)}, u32[]{:S(2)}) collective-permute-start(f32[256,128]{1,0:T(8,128)S(1)} %get-tuple-element.559), channel_id=1, source_target_pairs={{16,0},{32,16},{48,32},{64,48},{80,64},{96,80},{112,96},{128,112},... | collective-permute-start | bytes 393224 | tf_op jit(solution)/shard_map/while/body/eval_jaxpr/ppermute | solution.py:11
  673.1 8.2 %collective-permute-start.1 = (f32[256,128]{1,0:T(8,128)S(1)}, f32[256,128]{1,0:T(8,128)S(1)}, u32[]{:S(2)}, u32[]{:S(2)}) collective-permute-start(f32[256,128]{1,0:T(8,128)S(1)} %get-tuple-element.559), channel_id=1, source_target_pairs={{16,0},{32,16},{48,32},{64,48},{80,64},{96,80},{112,96},{128,112},... | collective-permute-start | bytes 393224 | tf_op jit(solution)/shard_map/while/body/eval_jaxpr/ppermute | solution.py:11
  681.3 7.4 %collective-permute-start.1 = (f32[256,128]{1,0:T(8,128)S(1)}, f32[256,128]{1,0:T(8,128)S(1)}, u32[]{:S(2)}, u32[]{:S(2)}) collective-permute-start(f32[256,128]{1,0:T(8,128)S(1)} %get-tuple-element.559), channel_id=1, source_target_pairs={{16,0},{32,16},{48,32},{64,48},{80,64},{96,80},{112,96},{128,112},... | collective-permute-start | bytes 393224 | tf_op jit(solution)/shard_map/while/body/eval_jaxpr/ppermute | solution.py:11
  688.8 7.1 %collective-permute-start.1 = (f32[256,128]{1,0:T(8,128)S(1)}, f32[256,128]{1,0:T(8,128)S(1)}, u32[]{:S(2)}, u32[]{:S(2)}) collective-permute-start(f32[256,128]{1,0:T(8,128)S(1)} %get-tuple-element.559), channel_id=1, source_target_pairs={{16,0},{32,16},{48,32},{64,48},{80,64},{96,80},{112,96},{128,112},... | collective-permute-start | bytes 393224 | tf_op jit(solution)/shard_map/while/body/eval_jaxpr/ppermute | solution.py:11
Sparse Core Ops, SparseCore 0:
  191.5 78.5 reduce-scatter.1
  276.3 250.3 all-reduce.2
  530.0 48.5 all-gather.1
where the time goes:
time: 706 us; the launch traced here: 704 us
  waiting for transfers between devices  401 us (57%)
  matrix products  114 us (16%)
  blocking collectives  74.1 us (10%)
  starting transfers between devices  55.1 us (8%)
  local copies, waits for them, and re-layouts  29.7 us (4%)
  other arithmetic  14.1 us (2%)
  between operations  13.9 us (2%)
    psum x1, waiting for transfers between devices, per_device(): lax.psum((jnp.einsum('nf,nh->fh', features, grad_pre, preferred_element_t...  177 us
    ppermute x30, waiting for transfers between devices, shifted(): return lax.ppermute(block, axis, route)  96.3 us
    reduce_scatter x1, waiting for transfers between devices, per_device(): lax.psum_scatter(running.reshape(row_blocks * tile_size, feat_width), 're...  77.7 us
    psum x1, blocking collectives, per_device(): lax.psum((jnp.einsum('nf,nh->fh', features, grad_pre, preferred_element_t...  74.1 us
    ppermute x30, starting transfers between devices, shifted(): return lax.ppermute(block, axis, route)  55 us
    all_gather x1, waiting for transfers between devices, per_device(): lax.all_gather(grad_agg, 'rep', axis=0, tiled=True)  50.3 us
    dot_general x16, matrix products, gather_term(): jnp.einsum('td,tif->dif', pick_entry(place_all, source), product, precisi...  43.8 us
    dot_general x16, matrix products, spread_term(): jnp.einsum('tij,tif->tjf', tile_part, chosen, preferred_element_type=jnp....  22.8 us
  transfers between devices with their start and end apart: 33, of which 18 were waited for; matrix products, arithmetic and copies ran while one was open for 9% of the time, Pallas kernels for 0%

commit v1 on v0

--- a/solution.py
+++ b/solution.py
@@ -72,9 +72,9 @@
     grad_agg = (
         jnp.einsum("nh,fh->nf", grad_pre, w_neigh, preferred_element_type=jnp.float32) / degree_f
     ).astype(jnp.bfloat16)
-    grad_whole = lax.all_gather(grad_agg, "rep", axis=0, tiled=True).reshape(
-        row_blocks, tile_size, feat_width
-    )
+    grad_whole = jnp.concatenate(
+        lax.all_to_all(jnp.stack([grad_agg] * lax.axis_size("rep")), "rep", 0, 0), axis=0
+    ).reshape(row_blocks, tile_size, feat_width)
     node_total = row_count * loop_count * rep_count
     grad_scale = 1.0 / math.sqrt(node_total)
     grad_self, grad_neigh, grad_bias = lax.psum(

time: 706 us -> 665 us (0.942)
  waiting for transfers between devices: 401 us -> 351 us
    all_gather x1 -> x0, waiting for transfers between devices: 50.3 us -> none  [per_device(): lax.all_gather(grad_agg, 'rep', axis=0, tiled=True)]
  transfers between devices with their start and end apart: 33 -> 33, of which waited for: 18 -> 17; matrix products, arithmetic and copies ran while one was open for 9% -> 10% of each run, Pallas kernels for 0% -> 0%
where the time goes in v1:
time: 665 us; the launch traced here: 663 us
  waiting for transfers between devices  351 us (53%)
  matrix products  113 us (17%)
  blocking collectives  80.1 us (12%)
  starting transfers between devices  59 us (9%)
  local copies, waits for them, and re-layouts  29.4 us (4%)
  other arithmetic  14.2 us (2%)
  between operations  14.2 us (2%)
    psum x1, waiting for transfers between devices, per_device(): lax.psum((jnp.einsum('nf,nh->fh', features, grad_pre, preferred_element_t...  177 us
    ppermute x30, waiting for transfers between devices, shifted(): return lax.ppermute(block, axis, route)  96.3 us
    psum x1, blocking collectives, per_device(): lax.psum((jnp.einsum('nf,nh->fh', features, grad_pre, preferred_element_t...  80.1 us
    reduce_scatter x1, waiting for transfers between devices, per_device(): lax.psum_scatter(running.reshape(row_blocks * tile_size, feat_width), 're...  77.2 us
    ppermute x30, starting transfers between devices, shifted(): return lax.ppermute(block, axis, route)  53.5 us
    dot_general x16, matrix products, gather_term(): jnp.einsum('td,tif->dif', pick_entry(place_all, source), product, precisi...  43.8 us
    dot_general x16, matrix products, spread_term(): jnp.einsum('tij,tif->tjf', tile_part, chosen, preferred_element_type=jnp....  22.8 us
    dot_general x16, matrix products, gather_term(): jnp.einsum('tij,tjf->tif', tile_part, chosen, preferred_element_type=jnp....  22.6 us
  transfers between devices with their start and end apart: 33, of which 17 were waited for; matrix products, arithmetic and copies ran while one was open for 10% of the time, Pallas kernels for 0%

profile of v1, /device:TPU:2, one launch (start us, length us, event | category | flops | bytes accessed | tf_op | source)
XLA Modules:
  0.0 662.6 jit_solution(9859981537833282876)
XLA Ops:
  9.5 1.5 gather_fusion.2
  13.3 1.5 fusion.33
  14.8 174.0 %while.32 = (s32[]{:T(128)}, bf16[256,128]{1,0:T(8,128)(2,1)S(1)}, f32[32,128,128]{2,0,1:T(8,128)S(1)}, s32[]{:T(128)}, f32[16,16,32]{2,1,0:T(8,128)S(1)}, /*ind...) while((s32[]{:T(128)}, bf16[256,128]{1,0:T(8,128)(2,1)S(1)}, ...), condition=%wide.region_1.3_spmd, body=%wide.region_0.2_spmd.sunk | while | flops 168559728 | bytes 8794716 | solution.py:56
  14.8 1.7 collective-permute-start
  16.5 7.5 %collective-permute-done = bf16[256,128]{1,0:T(8,128)(2,1)S(1)} collective-permute-done((bf16[256,128]{1,0:T(8,128)(2,1)S(1)}, bf16[256,128]{1,0:T(8,128)(2,1)S(1)}, u32[]{:S(2)}, u32[]{:S(2)}) %collective-permute-start) | collective-permute-done | bytes 65568 | tf_op jit(solution)/shard_map/while/body/eval_jaxpr/ppermute | solution.py:11
  26.1 2.8 convolution_add_fusion.4
  29.1 6.3 collective-permute-done
  37.5 2.8 convolution_add_fusion.4
  40.5 6.3 collective-permute-done
  48.9 2.8 convolution_add_fusion.4
  51.9 6.3 collective-permute-done
  60.2 2.8 convolution_add_fusion.4
  63.2 6.3 collective-permute-done
  71.6 2.8 convolution_add_fusion.4
  74.6 6.3 collective-permute-done
  83.0 2.8 convolution_add_fusion.4
  86.0 6.3 collective-permute-done
  94.4 2.8 convolution_add_fusion.4
  97.4 6.3 collective-permute-done
  105.8 2.8 convolution_add_fusion.4
  108.8 6.8 %collective-permute-done = bf16[256,128]{1,0:T(8,128)(2,1)S(1)} collective-permute-done((bf16[256,128]{1,0:T(8,128)(2,1)S(1)}, bf16[256,128]{1,0:T(8,128)(2,1)S(1)}, u32[]{:S(2)}, u32[]{:S(2)}) %collective-permute-start) | collective-permute-done | bytes 65568 | tf_op jit(solution)/shard_map/while/body/eval_jaxpr/ppermute | solution.py:11
  117.7 2.8 convolution_add_fusion.4
  120.7 6.3 collective-permute-done
  129.1 2.8 convolution_add_fusion.4
  132.1 6.3 collective-permute-done
  140.5 2.8 convolution_add_fusion.4
  143.5 6.3 collective-permute-done
  151.8 2.8 convolution_add_fusion.4
  154.8 6.3 collective-permute-done
  163.2 2.8 convolution_add_fusion.4
  166.2 6.3 collective-permute-done
  174.6 2.8 convolution_add_fusion.4
  177.6 6.3 collective-permute-done
  186.0 2.8 convolution_add_fusion.4
  188.8 2.6 copy.18
  193.0 77.2 %reduce-scatter.2.cloned.1.call-done = f32[256,128]{1,0:T(8,128)} async-done(((f32[4096,128]{1,0:T(8,128)}), f32[256,128]{1,0:T(8,128)}) %reduce-scatter.2.cloned.1.call-update) | async-done | bytes 131088 | tf_op jit(solution)/shard_map/reduce_scatter | solution.py:57
  270.1 1.9 convert_reduce_fusion
  273.4 5.5 all-to-all-start
  280.9 80.1 %psum.23 = f32[256]{0:T(256)} all-reduce(f32[256]{0:T(256)S(1)} %broadcast_multiply_fusion), channel_id=1, replica_groups=mesh['loop'=16,'rep'=16] {'loop','rep'}, use_global_device_ids=true, to_apply=%region_8.11 | all-reduce | flops 256 | bytes 2048 | tf_op jit(solution)/shard_map/psum | solution.py:80
  361.0 177.1 %all-reduce.3.cloned.1.call-done = (f32[128,256]{0,1:T(8,128)}, f32[128,256]{1,0:T(8,128)}) async-done(((f32[128,256]{0,1:T(8,128)}, f32[128,256]{1,0:T(8,128)}), (f32[128,256]{0,1:T(8,128)}, f32[128,256]{1,0:T(8,128)})) %all-reduce.3.cloned.1.call-update) | async-done | bytes 262160 | tf_op jit(solution)/shard_map/psum | solution.py:80
  538.1 1.7 copy.20
  542.9 111.3 %while.33 = (s32[]{:T(128)}, f32[256,128]{1,0:T(8,128)S(1)}, s32[]{:T(128)}, f32[16,16,2]{1,2,0:T(2,128)S(1)}, bf16[16,16,128,128]{3,2,1,0:T(8,128)(2,1)}, /*ind...) while((s32[]{:T(128)}, f32[256,128]{1,0:T(8,128)S(1)}, ...), condition=%wide.region_4.7_spmd, body=%wide.region_3.6_spmd.sunk | while | flops 73696368 | bytes 5510748 | solution.py:105
  545.6 1.4 fusion.93
  548.3 4.2 collective-permute-start.1
  556.6 3.7 collective-permute-start.1
  561.7 1.4 fusion.93
  564.4 3.1 collective-permute-start.1
  568.9 1.4 fusion.93
  571.5 3.1 collective-permute-start.1
  576.0 1.4 fusion.93
  578.7 3.1 collective-permute-start.1
  585.9 3.6 collective-permute-start.1
  590.9 1.4 fusion.93
  593.6 4.3 collective-permute-start.1
  599.3 1.4 fusion.93
  601.9 3.5 collective-permute-start.1
  609.5 3.1 collective-permute-start.1
  614.0 1.4 fusion.93
  616.6 3.1 collective-permute-start.1
  623.8 3.1 collective-permute-start.1
  631.0 4.0 collective-permute-start.1
  636.3 1.4 fusion.93
  639.0 4.0 collective-permute-start.1
  647.1 3.1 collective-permute-start.1
  (247 shorter events, 96.2 us)
Async XLA Ops:
  7.2 263.0 %copy-start = (bf16[128,256]{1,0:T(8,128)(2,1)S(1)}, bf16[128,256]{1,0:T(8,128)(2,1)}, u32[]{:S(2)}) copy-start(bf16[128,256]{1,0:T(8,128)(2,1)} %param.20) | copy-start | bytes 196612
  7.2 262.9 %reduce-scatter.2.cloned.1.call-start = ((), (), s32[]{:S(2)}) async-start(), calls=%async_computation.2 | async-start | bytes 2228224 | tf_op jit(solution)/shard_map/reduce_scatter | solution.py:57
  13.3 1.5 copy-start.4
  14.8 9.2 %collective-permute-start = (bf16[256,128]{1,0:T(8,128)(2,1)S(1)}, bf16[256,128]{1,0:T(8,128)(2,1)S(1)}, u32[]{:S(2)}, u32[]{:S(2)}) collective-permute-start(bf16[256,128]{1,0:T(8,128)(2,1)S(1)} %get-tuple-element.526), channel_id=1, source_target_pairs={{240,0},{0,16},{16,32},{32,48},{48,64},{64,80},{80,96},{96,112},{1... | collective-permute-start | bytes 196616 | tf_op jit(solution)/shard_map/while/body/eval_jaxpr/ppermute | solution.py:11
  28.9 6.5 collective-permute-start
  40.3 6.5 collective-permute-start
  51.7 6.5 collective-permute-start
  63.1 6.5 collective-permute-start
  74.5 6.5 collective-permute-start
  85.9 6.5 collective-permute-start
  97.3 6.5 collective-permute-start
  108.6 7.0 %collective-permute-start = (bf16[256,128]{1,0:T(8,128)(2,1)S(1)}, bf16[256,128]{1,0:T(8,128)(2,1)S(1)}, u32[]{:S(2)}, u32[]{:S(2)}) collective-permute-start(bf16[256,128]{1,0:T(8,128)(2,1)S(1)} %get-tuple-element.526), channel_id=1, source_target_pairs={{240,0},{0,16},{16,32},{32,48},{48,64},{64,80},{80,96},{96,112},{1... | collective-permute-start | bytes 196616 | tf_op jit(solution)/shard_map/while/body/eval_jaxpr/ppermute | solution.py:11
  120.5 6.5 collective-permute-start
  131.9 6.5 collective-permute-start
  143.3 6.5 collective-permute-start
  154.7 6.5 collective-permute-start
  166.1 6.5 collective-permute-start
  177.5 6.5 collective-permute-start
  191.4 0.7 copy-start.5
  191.4 1.4 copy-start.1
  191.4 1.4 copy-start.2
  191.4 78.7 %copy-start.6 = (bf16[256,256]{1,0:T(8,128)(2,1)S(1)}, bf16[256,256]{1,0:T(8,128)(2,1)}, u32[]{:S(2)}) copy-start(bf16[256,256]{1,0:T(8,128)(2,1)} %param.27) | copy-start | bytes 393220
  191.4 78.7 %copy-start.8 = (f32[256]{0:T(256)S(1)}, f32[256]{0:T(256)}, u32[]{:S(2)}) copy-start(f32[256]{0:T(256)} %param.21) | copy-start | bytes 3076
  272.0 7.8 %copy-start.7 = (f32[256,128]{1,0:T(8,128)S(1)}, f32[256,128]{1,0:T(8,128)}, u32[]{:S(2)}) copy-start(f32[256,128]{1,0:T(8,128)} %reduce-scatter.2.cloned.1.call-done) | copy-start | bytes 393220
  273.4 266.3 %all-to-all-start = ((bf16[16,256,128]{2,1,0:T(8,128)(2,1)}), bf16[16,256,128]{2,1,0:T(8,128)(2,1)S(1)}, u32[]{:S(2)}, u32[]{:S(2)}) async-start(bf16[16,256,128]{2,1,0:T(8,128)(2,1)} %stack.2), calls=%async_computation.1 | async-start | bytes 2097152 | tf_op jit(solution)/shard_map/all_to_all | solution.py:76
  278.9 259.2 %all-reduce.3.cloned.1.call-start = ((), (), s32[]{:S(2)}) async-start(), calls=%async_computation.3 | async-start | bytes 524288 | tf_op jit(solution)/shard_map/psum | solution.py:80
  542.9 112.1 %copy-start.3 = (f32[128,256]{1,0:T(8,128)S(1)}, f32[128,256]{1,0:T(8,128)}, u32[]{:S(2)}) copy-start(f32[128,256]{1,0:T(8,128)} %get-tuple-element.583) | copy-start | bytes 393220
  542.9 5.3 collective-permute-start.1
  548.3 8.2 %collective-permute-start.1 = (f32[256,128]{1,0:T(8,128)S(1)}, f32[256,128]{1,0:T(8,128)S(1)}, u32[]{:S(2)}, u32[]{:S(2)}) collective-permute-start(f32[256,128]{1,0:T(8,128)S(1)} %get-tuple-element.559), channel_id=1, source_target_pairs={{16,0},{32,16},{48,32},{64,48},{80,64},{96,80},{112,96},{128,112},... | collective-permute-start | bytes 393224 | tf_op jit(solution)/shard_map/while/body/eval_jaxpr/ppermute | solution.py:11
  556.6 7.7 %collective-permute-start.1 = (f32[256,128]{1,0:T(8,128)S(1)}, f32[256,128]{1,0:T(8,128)S(1)}, u32[]{:S(2)}, u32[]{:S(2)}) collective-permute-start(f32[256,128]{1,0:T(8,128)S(1)} %get-tuple-element.559), channel_id=1, source_target_pairs={{16,0},{32,16},{48,32},{64,48},{80,64},{96,80},{112,96},{128,112},... | collective-permute-start | bytes 393224 | tf_op jit(solution)/shard_map/while/body/eval_jaxpr/ppermute | solution.py:11
  564.4 7.1 %collective-permute-start.1 = (f32[256,128]{1,0:T(8,128)S(1)}, f32[256,128]{1,0:T(8,128)S(1)}, u32[]{:S(2)}, u32[]{:S(2)}) collective-permute-start(f32[256,128]{1,0:T(8,128)S(1)} %get-tuple-element.559), channel_id=1, source_target_pairs={{16,0},{32,16},{48,32},{64,48},{80,64},{96,80},{112,96},{128,112},... | collective-permute-start | bytes 393224 | tf_op jit(solution)/shard_map/while/body/eval_jaxpr/ppermute | solution.py:11
  571.5 7.1 %collective-permute-start.1 = (f32[256,128]{1,0:T(8,128)S(1)}, f32[256,128]{1,0:T(8,128)S(1)}, u32[]{:S(2)}, u32[]{:S(2)}) collective-permute-start(f32[256,128]{1,0:T(8,128)S(1)} %get-tuple-element.559), channel_id=1, source_target_pairs={{16,0},{32,16},{48,32},{64,48},{80,64},{96,80},{112,96},{128,112},... | collective-permute-start | bytes 393224 | tf_op jit(solution)/shard_map/while/body/eval_jaxpr/ppermute | solution.py:11
  578.7 7.1 %collective-permute-start.1 = (f32[256,128]{1,0:T(8,128)S(1)}, f32[256,128]{1,0:T(8,128)S(1)}, u32[]{:S(2)}, u32[]{:S(2)}) collective-permute-start(f32[256,128]{1,0:T(8,128)S(1)} %get-tuple-element.559), channel_id=1, source_target_pairs={{16,0},{32,16},{48,32},{64,48},{80,64},{96,80},{112,96},{128,112},... | collective-permute-start | bytes 393224 | tf_op jit(solution)/shard_map/while/body/eval_jaxpr/ppermute | solution.py:11
  585.9 7.6 %collective-permute-start.1 = (f32[256,128]{1,0:T(8,128)S(1)}, f32[256,128]{1,0:T(8,128)S(1)}, u32[]{:S(2)}, u32[]{:S(2)}) collective-permute-start(f32[256,128]{1,0:T(8,128)S(1)} %get-tuple-element.559), channel_id=1, source_target_pairs={{16,0},{32,16},{48,32},{64,48},{80,64},{96,80},{112,96},{128,112},... | collective-permute-start | bytes 393224 | tf_op jit(solution)/shard_map/while/body/eval_jaxpr/ppermute | solution.py:11
  593.6 8.3 %collective-permute-start.1 = (f32[256,128]{1,0:T(8,128)S(1)}, f32[256,128]{1,0:T(8,128)S(1)}, u32[]{:S(2)}, u32[]{:S(2)}) collective-permute-start(f32[256,128]{1,0:T(8,128)S(1)} %get-tuple-element.559), channel_id=1, source_target_pairs={{16,0},{32,16},{48,32},{64,48},{80,64},{96,80},{112,96},{128,112},... | collective-permute-start | bytes 393224 | tf_op jit(solution)/shard_map/while/body/eval_jaxpr/ppermute | solution.py:11
  601.9 7.5 %collective-permute-start.1 = (f32[256,128]{1,0:T(8,128)S(1)}, f32[256,128]{1,0:T(8,128)S(1)}, u32[]{:S(2)}, u32[]{:S(2)}) collective-permute-start(f32[256,128]{1,0:T(8,128)S(1)} %get-tuple-element.559), channel_id=1, source_target_pairs={{16,0},{32,16},{48,32},{64,48},{80,64},{96,80},{112,96},{128,112},... | collective-permute-start | bytes 393224 | tf_op jit(solution)/shard_map/while/body/eval_jaxpr/ppermute | solution.py:11
  609.5 7.1 %collective-permute-start.1 = (f32[256,128]{1,0:T(8,128)S(1)}, f32[256,128]{1,0:T(8,128)S(1)}, u32[]{:S(2)}, u32[]{:S(2)}) collective-permute-start(f32[256,128]{1,0:T(8,128)S(1)} %get-tuple-element.559), channel_id=1, source_target_pairs={{16,0},{32,16},{48,32},{64,48},{80,64},{96,80},{112,96},{128,112},... | collective-permute-start | bytes 393224 | tf_op jit(solution)/shard_map/while/body/eval_jaxpr/ppermute | solution.py:11
  616.6 7.1 %collective-permute-start.1 = (f32[256,128]{1,0:T(8,128)S(1)}, f32[256,128]{1,0:T(8,128)S(1)}, u32[]{:S(2)}, u32[]{:S(2)}) collective-permute-start(f32[256,128]{1,0:T(8,128)S(1)} %get-tuple-element.559), channel_id=1, source_target_pairs={{16,0},{32,16},{48,32},{64,48},{80,64},{96,80},{112,96},{128,112},... | collective-permute-start | bytes 393224 | tf_op jit(solution)/shard_map/while/body/eval_jaxpr/ppermute | solution.py:11
  623.8 7.1 %collective-permute-start.1 = (f32[256,128]{1,0:T(8,128)S(1)}, f32[256,128]{1,0:T(8,128)S(1)}, u32[]{:S(2)}, u32[]{:S(2)}) collective-permute-start(f32[256,128]{1,0:T(8,128)S(1)} %get-tuple-element.559), channel_id=1, source_target_pairs={{16,0},{32,16},{48,32},{64,48},{80,64},{96,80},{112,96},{128,112},... | collective-permute-start | bytes 393224 | tf_op jit(solution)/shard_map/while/body/eval_jaxpr/ppermute | solution.py:11
  631.0 8.0 %collective-permute-start.1 = (f32[256,128]{1,0:T(8,128)S(1)}, f32[256,128]{1,0:T(8,128)S(1)}, u32[]{:S(2)}, u32[]{:S(2)}) collective-permute-start(f32[256,128]{1,0:T(8,128)S(1)} %get-tuple-element.559), channel_id=1, source_target_pairs={{16,0},{32,16},{48,32},{64,48},{80,64},{96,80},{112,96},{128,112},... | collective-permute-start | bytes 393224 | tf_op jit(solution)/shard_map/while/body/eval_jaxpr/ppermute | solution.py:11
  639.0 8.0 %collective-permute-start.1 = (f32[256,128]{1,0:T(8,128)S(1)}, f32[256,128]{1,0:T(8,128)S(1)}, u32[]{:S(2)}, u32[]{:S(2)}) collective-permute-start(f32[256,128]{1,0:T(8,128)S(1)} %get-tuple-element.559), channel_id=1, source_target_pairs={{16,0},{32,16},{48,32},{64,48},{80,64},{96,80},{112,96},{128,112},... | collective-permute-start | bytes 393224 | tf_op jit(solution)/shard_map/while/body/eval_jaxpr/ppermute | solution.py:11
  647.1 7.1 %collective-permute-start.1 = (f32[256,128]{1,0:T(8,128)S(1)}, f32[256,128]{1,0:T(8,128)S(1)}, u32[]{:S(2)}, u32[]{:S(2)}) collective-permute-start(f32[256,128]{1,0:T(8,128)S(1)} %get-tuple-element.559), channel_id=1, source_target_pairs={{16,0},{32,16},{48,32},{64,48},{80,64},{96,80},{112,96},{128,112},... | collective-permute-start | bytes 393224 | tf_op jit(solution)/shard_map/while/body/eval_jaxpr/ppermute | solution.py:11
Sparse Core Ops, SparseCore 0:
  191.6 78.5 reduce-scatter.1
  285.9 252.1 all-reduce.2
